TPU v7x, 256 devices: a whole 4x4x8 slice. The times are simulated.
256 devices in a mesh: row: 16 (over x, y_hi, core), col: 16 (over y_lo, z).
Axes of the slice: x: 4, y: 4 (y_hi: 2, y_lo: 2; y = y_hi * 2 + y_lo), z: 8, core: 2. Of those that a mesh axis runs over, the one named last changes fastest.
Arguments:
- query_in: bfloat16 [4096, 8192], P('row', 'col'), may hold values from -6 to 6
- key_in: bfloat16 [4096, 8192], P('row', 'col'), may hold values from -6 to 6
- value_in: bfloat16 [4096, 8192], P('row', 'col'), may hold values from -6 to 6
- filters: float32 [512, 128], P('col'), may hold values from -0.5 to 0.5
- out_weight: bfloat16 [8192, 8192], P('row', 'col'), may hold values from -0.0625 to 0.0625
- out_grad: bfloat16 [4096, 8192], P('row', 'col'), may hold values from -6 to 6
Outputs:
- mixed: bfloat16 [4096, 8192], P('row', 'col')
- query_grad: bfloat16 [4096, 8192], P('row', 'col')
- key_grad: bfloat16 [4096, 8192], P('row', 'col')
- value_grad: bfloat16 [4096, 8192], P('row', 'col')
- weight_grad: bfloat16 [8192, 8192], P('row', 'col')
- filter_grad: float32 [512, 128], P('col')
All inputs are finite; a program needn't handle non-finite values.
Results may differ from a plain program's by a relative error of at most 0.018.
Values may be sent and summed in bfloat16 or wider, within the bound.
A program may use at most 128 MiB of HBM per device.

v0:
```python
import math
import jax
import jax.numpy as jnp
from jax import lax
from jax.sharding import PartitionSpec as P


def from_behind(shard, axis, by):
    size = lax.axis_size(axis)
    pairs = [(i, i + by) for i in range(size) if 0 <= i + by < size]
    return lax.ppermute(shard, axis, pairs)


def toeplitz(taps, causal):
    groups, span = taps.shape
    if causal:
        template = jnp.concatenate(
            [
                jnp.zeros((groups, 1), jnp.float32),
                taps[:, ::-1],
                jnp.zeros((groups, span), jnp.float32),
            ],
            1,
        )
    else:
        template = jnp.concatenate([taps, jnp.zeros((groups, span + 1), jnp.float32)], 1)
    tiled = jnp.tile(template, (1, span))
    return tiled[:, : 2 * span * span].reshape(groups, span, 2 * span)


def windows(extended, span):
    count = (extended.shape[0] - span) // span
    first = extended[:-span].reshape(count, span, extended.shape[1])
    second = extended[span:].reshape(count, span, extended.shape[1])
    return jnp.concatenate([first, second], axis=1)


def convolve(matrix, extended, span, group):
    blocks = windows(extended, span)
    count, _, width = blocks.shape
    split = blocks.reshape(count, 2 * span, width // group, group)
    result = jnp.einsum("gts,bsgc->btgc", matrix, split, precision=lax.Precision.HIGHEST)
    return result.reshape(count * span, width)


def shards(query_in, key_in, value_in, filters, out_weight, out_grad):
    f32 = jnp.float32
    bf16 = jnp.bfloat16
    tokens, width = query_in.shape
    span = filters.shape[1]
    group = width // filters.shape[0]
    total_tokens = tokens * lax.axis_size("row")
    key32 = key_in.astype(f32)
    value32 = value_in.astype(f32)
    query32 = query_in.astype(f32)
    product = key32 * value32
    key_rim, value_rim = from_behind((key_in[-span:], value_in[-span:]), "row", 1)
    product_rim = key_rim.astype(f32) * value_rim.astype(f32)
    product_ext = jnp.concatenate([product_rim, product], 0)
    conv = convolve(toeplitz(filters, True), product_ext, span, group)
    gated = (query32 * conv).astype(bf16)
    panel = lax.all_gather(gated, "col", axis=1, tiled=True)
    weights = lax.all_gather(out_weight, "row", axis=0, tiled=True)
    mixed_sum = jnp.dot(panel, weights, preferred_element_type=f32)
    partial_value = lax.dot_general(
        out_grad, weights, (((1,), (1,)), ((), ())), preferred_element_type=f32
    )
    mixed = mixed_sum.astype(bf16)
    grad_gated = lax.psum_scatter(
        partial_value.astype(jnp.bfloat16), "col", scatter_dimension=1, tiled=True
    ).astype(jnp.float32)
    query_grad = (grad_gated * conv).astype(bf16)
    grad_conv = grad_gated * query32
    grad_rim = from_behind(grad_conv[:span].astype(jnp.bfloat16), "row", -1).astype(jnp.float32)
    grad_ext = jnp.concatenate([grad_conv, grad_rim], 0)
    grad_product = convolve(toeplitz(filters, False), grad_ext, span, group)
    key_grad = (grad_product * value32).astype(bf16)
    value_grad = (grad_product * key32).astype(bf16)
    count = tokens // span
    groups = width // group
    grad_blocks = grad_conv.reshape(count, span, groups, group)
    product_blocks = windows(product_ext, span).reshape(count, 2 * span, groups, group)
    corr = jnp.einsum(
        "btgc,bsgc->gts", grad_blocks, product_blocks, precision=lax.Precision.HIGHEST
    )
    flat = jnp.concatenate(
        [corr.reshape(groups, 2 * span * span), jnp.zeros((groups, span), f32)], 1
    )
    skewed = flat.reshape(groups, span, 2 * span + 1)[:, :, 1 : span + 1]
    local_taps = jnp.sum(skewed, axis=1)[:, ::-1]
    filter_grad = lax.psum(local_taps, "row") * (1.0 / math.sqrt(total_tokens * group))
    weight_sum = lax.psum_scatter(
        lax.dot_general(
            panel, out_grad, (((0,), (0,)), ((), ())), preferred_element_type=f32
        ).astype(jnp.bfloat16),
        "row",
        scatter_dimension=0,
        tiled=True,
    ).astype(jnp.float32)
    weight_grad = (weight_sum * (1.0 / math.sqrt(total_tokens))).astype(bf16)
    return (mixed, query_grad, key_grad, value_grad, weight_grad, filter_grad)


def solution(mesh):
    placed = (
        P("row", "col"),
        P("row", "col"),
        P("row", "col"),
        P("col", None),
        P("row", "col"),
        P("row", "col"),
    )
    return jax.shard_map(
        shards,
        mesh=mesh,
        in_specs=placed,
        out_specs=(
            P("row", "col"),
            P("row", "col"),
            P("row", "col"),
            P("row", "col"),
            P("row", "col"),
            P("col", None),
        ),
        check_vma=False,
    )
```

profile of v0, /device:TPU:2, one launch (start us, length us, event | category | flops | bytes accessed | tf_op | source)
XLA Modules:
  0.0 399.6 jit_solution(14120310710008545654)
XLA Ops:
  7.2 0.7 all-gather.5.cloned.1.call-update
  8.0 82.3 %all-gather.5.cloned.1.call-done = bf16[8192,512]{1,0:T(8,128)(2,1)} async-done(((bf16[512,512]{1,0:T(8,128)(2,1)}), bf16[8192,512]{1,0:T(8,128)(2,1)}) %all-gather.5.cloned.1.call-update) | async-done | bytes 8388624 | tf_op jit(solution)/shard_map/all_gather | solution.py:63
  90.2 7.8 %convolution_convert_fusion.1 = bf16[256,8192]{1,0:T(8,128)(2,1)} fusion(bf16[256,512]{1,0:T(8,128)(2,1)S(1)} %copy-done, bf16[8192,512]{1,0:T(8,128)(2,1)} %all-gather.5.cloned.1.call-done), kind=kOutput, calls=%fused_computation.1 | convolution fusion | flops 2149580800 | bytes 12845056 | tf_op jit(solution)/shard_map/dot_general | solution.py:65
  98.1 0.9 copy-done.6
  99.2 2.1 collective-permute-start
  101.3 0.1 copy.16
  101.5 2.3 collective-permute-start.1
  103.9 3.1 tile.20
  107.0 6.7 %tile.21 = f32[32,32896]{1,0:T(8,128)} reshape(f32[32,128,257]{2,1,0:T(8,128)} %tile.20) | data formatting | bytes 8421376 | tf_op jit(solution)/shard_map/tile | solution.py:27
  113.7 2.2 slice-done
  115.9 3.3 copy.37
  119.4 3.1 tile.8
  122.5 6.7 %tile.9 = f32[32,32896]{1,0:T(8,128)} reshape(f32[32,128,257]{2,1,0:T(8,128)} %tile.8) | data formatting | bytes 8421376 | tf_op jit(solution)/shard_map/tile | solution.py:27
  129.2 2.2 slice-done.1
  131.4 3.2 copy.35
  134.6 44.5 %reduce-scatter.3.cloned.1.call-done = bf16[256,512]{1,0:T(8,128)(2,1)} async-done(((bf16[256,8192]{1,0:T(8,128)(2,1)}), bf16[256,512]{1,0:T(8,128)(2,1)}) %reduce-scatter.3.cloned.1.call-update) | async-done | bytes 262160 | tf_op jit(solution)/shard_map/reduce_scatter | solution.py:69
  179.1 1.0 convert_multiply_fusion
  180.2 0.7 slice.42
  180.8 2.1 collective-permute-start.2
  183.0 0.2 copy.24
  183.2 0.3 concatenate.37
  183.5 2.0 collective-permute-done.2
  185.6 0.2 copy.25
  185.8 0.3 concatenate.39
  186.2 5.9 %fusion.7 = f32[2,128,32,16]{1,3,0,2:T(8,128)S(1)} fusion(f32[32,128,256,1]{2,1,0,3:T(8,128)} %bitcast.60, f32[2,128,32,16]{1,3,0,2:T(8,128)S(1)} %copy.27, f32[2,128,32,16]{1,3,0,2:T(8,128)S(1)} %copy.26), kind=kOutput, calls=%fused_computation.8 | convolution fusion | flops 402915328 | bytes 5767168 | tf_op jit(solution)/shard_map/gts,bsgc->btgc/dot_general | solution.py:42
  192.1 0.3 copy.28
  192.4 0.9 fusion.14
  193.3 0.3 concatenate.34
  193.6 0.3 concatenate.33
  194.0 5.9 %fusion.4 = f32[2,128,32,16]{1,3,0,2:T(8,128)S(1)} fusion(f32[2,256,32,16]{1,3,0,2:T(8,128)S(1)} %copy_dynamic-update-slice_fusion, f32[32,128,256,1]{2,1,0,3:T(8,128)} %bitcast.59), kind=kOutput, calls=%fused_computation.7 | convolution fusion | flops 402653184 | bytes 5767168 | tf_op jit(solution)/shard_map/gts,bsgc->btgc/dot_general | solution.py:42
  200.0 0.3 copy.21
  200.3 0.2 copy.22
  200.5 0.9 fusion.16
  201.4 0.3 reduce-scatter.5.cloned.1.call-start
  201.7 73.7 %all-gather.3.cloned.1.call-done = bf16[256,8192]{1,0:T(8,128)(2,1)} async-done(((bf16[256,512]{1,0:T(8,128)(2,1)}), bf16[256,8192]{1,0:T(8,128)(2,1)}) %all-gather.3.cloned.1.call-update) | async-done | bytes 4194320 | tf_op jit(solution)/shard_map/all_gather | solution.py:62
  275.4 7.8 %convolution_convert_fusion = bf16[8192,512]{1,0:T(8,128)(2,1)} fusion(bf16[256,8192]{1,0:T(8,128)(2,1)} %all-gather.3.cloned.1.call-done, bf16[256,512]{1,0:T(8,128)(2,1)S(1)} %copy-done), kind=kOutput, calls=%fused_computation | convolution fusion | flops 2151677952 | bytes 12845056 | tf_op jit(solution)/shard_map/dot_general | solution.py:93
  283.2 3.5 fusion.18
  286.7 2.4 copy.39
  289.2 2.3 concatenate.42
  291.5 8.2 %reshape.61 = f32[32,128,257]{2,1,0:T(8,128)} reshape(f32[32,32896]{1,0:T(8,128)} %concatenate.42) | data formatting | bytes 8421376 | tf_op jit(solution)/shard_map/reshape | solution.py:89
  299.7 3.2 slice_reduce_fusion
  303.0 0.8 copy.30
  303.9 0.8 copy.31
  304.7 57.5 %psum.7 = f32[32,128]{1,0:T(8,128)S(1)} all-reduce(f32[32,128]{1,0:T(8,128)S(1)} %rev.7), channel_id=1, replica_groups=mesh['row'=16,'col'=16] {'row'}, use_global_device_ids=true, to_apply=%region_3.0 | all-reduce | flops 4096 | bytes 32768 | tf_op jit(solution)/shard_map/psum | solution.py:91
  362.3 0.6 broadcast_multiply_fusion
  362.9 7.7 %convolution_convert_fusion.2 = bf16[256,512]{1,0:T(8,128)(2,1)} fusion(bf16[256,8192]{1,0:T(8,128)(2,1)} %all-gather.3.cloned.1.call-done, bf16[8192,512]{1,0:T(8,128)(2,1)} %all-gather.5.cloned.1.call-done), kind=kOutput, calls=%fused_computation.9 | convolution fusion | flops 2147614720 | bytes 12845056 | tf_op jit(solution)/shard_map/dot_general | solution.py:64
  370.6 20.6 %reduce-scatter.5.cloned.1.call-done = bf16[512,512]{1,0:T(8,128)(2,1)} async-done(((bf16[8192,512]{1,0:T(8,128)(2,1)}), bf16[512,512]{1,0:T(8,128)(2,1)}) %reduce-scatter.5.cloned.1.call-update) | async-done | bytes 524304 | tf_op jit(solution)/shard_map/reduce_scatter | solution.py:92
  391.2 1.9 multiply_convert_fusion
  (46 shorter events, 1.0 us)
Async XLA Ops:
  7.2 83.1 %copy-start = (bf16[256,512]{1,0:T(8,128)(2,1)S(1)}, bf16[256,512]{1,0:T(8,128)(2,1)}, u32[]{:S(2)}) copy-start(bf16[256,512]{1,0:T(8,128)(2,1)} %param.11) | copy-start | bytes 786436
  7.2 83.1 %all-gather.5.cloned.1.call-start = ((), (), s32[]{:S(2)}) async-start(), calls=%async_computation.3 | async-start | bytes 8912896 | tf_op jit(solution)/shard_map/all_gather | solution.py:63
  7.9 171.2 %reduce-scatter.3.cloned.1.call-start = ((), (), s32[]{:S(2)}) async-start(), calls=%async_computation.4 | async-start | bytes 4456448 | tf_op jit(solution)/shard_map/reduce_scatter | solution.py:69
  98.0 0.9 copy-start.6
  98.1 3.2 copy-start.7
  98.1 5.7 %copy-start.8 = (f32[32,128]{1,0:T(8,128)S(1)}, f32[32,128]{1,0:T(8,128)}, u32[]{:S(2)}) copy-start(f32[32,128]{1,0:T(8,128)} %param.9) | copy-start | bytes 49156
  98.1 177.3 %all-gather.3.cloned.1.call-start = ((), (), s32[]{:S(2)}) async-start(), calls=%async_computation.2 | async-start | bytes 4456448 | tf_op jit(solution)/shard_map/all_gather | solution.py:62
  99.2 83.8 %collective-permute-start = (bf16[128,512]{0,1:T(8,128)(2,1)S(1)}, bf16[128,512]{0,1:T(8,128)(2,1)S(1)}, u32[]{:S(2)}, u32[]{:S(2)}) collective-permute-start(bf16[128,512]{0,1:T(8,128)(2,1)S(1)} %slice.34), channel_id=1, source_target_pairs={{0,16},{16,32},{32,48},{48,64},{64,80},{80,96},{96,112},{112,128},... | collective-permute-start | bytes 393224 | tf_op jit(solution)/shard_map/ppermute | solution.py:11
  101.5 81.5 %collective-permute-start.1 = (bf16[128,512]{0,1:T(8,128)(2,1)S(1)}, bf16[128,512]{0,1:T(8,128)(2,1)S(1)}, u32[]{:S(2)}, u32[]{:S(2)}) collective-permute-start(bf16[128,512]{0,1:T(8,128)(2,1)S(1)} %slice.35), channel_id=1, source_target_pairs={{0,16},{16,32},{32,48},{48,64},{64,80},{80,96},{96,112},{112,128},... | collective-permute-start | bytes 393224 | tf_op jit(solution)/shard_map/ppermute | solution.py:11
  113.7 2.2 slice-start
  129.2 2.2 slice-start.1
  131.4 47.7 %copy-start.2 = (bf16[256,512]{1,0:T(8,128)(2,1)S(1)}, bf16[256,512]{1,0:T(8,128)(2,1)}, u32[]{:S(2)}) copy-start(bf16[256,512]{1,0:T(8,128)(2,1)} %param.6) | copy-start | bytes 786436
  180.8 4.7 %collective-permute-start.2 = (bf16[128,512]{1,0:T(8,128)(2,1)}, bf16[128,512]{1,0:T(8,128)(2,1)S(1)}, u32[]{:S(2)}, u32[]{:S(2)}) collective-permute-start(bf16[128,512]{1,0:T(8,128)(2,1)} %slice.42), channel_id=1, source_target_pairs={{16,0},{32,16},{48,32},{64,48},{80,64},{96,80},{112,96},{128,112},... | collective-permute-start | bytes 393224 | tf_op jit(solution)/shard_map/ppermute | solution.py:11
  194.0 6.5 %copy-start.3 = (bf16[256,512]{1,0:T(8,128)(2,1)S(1)}, bf16[256,512]{1,0:T(8,128)(2,1)}, u32[]{:S(2)}) copy-start(bf16[256,512]{1,0:T(8,128)(2,1)} %reduce-scatter.3.cloned.1.call-done) | copy-start | bytes 786436
  201.4 189.7 %reduce-scatter.5.cloned.1.call-start = ((), (), s32[]{:S(2)}) async-start(), calls=%async_computation.5 | async-start | bytes 8912896 | tf_op jit(solution)/shard_map/reduce_scatter | solution.py:92
  291.5 11.5 %copy-start.5 = (bf16[256,512]{0,1:T(8,128)(2,1)S(1)}, bf16[256,512]{0,1:T(8,128)(2,1)}, u32[]{:S(2)}) copy-start(bf16[256,512]{0,1:T(8,128)(2,1)} %get-tuple-element.13) | copy-start | bytes 786436
  291.5 12.4 %copy-start.4 = (bf16[256,512]{0,1:T(8,128)(2,1)S(1)}, bf16[256,512]{0,1:T(8,128)(2,1)}, u32[]{:S(2)}) copy-start(bf16[256,512]{0,1:T(8,128)(2,1)} %get-tuple-element.12) | copy-start | bytes 786436
  362.9 30.2 %copy-start.1 = (bf16[256,512]{1,0:T(8,128)(2,1)S(1)}, bf16[256,512]{1,0:T(8,128)(2,1)}, u32[]{:S(2)}) copy-start(bf16[256,512]{1,0:T(8,128)(2,1)} %param.11) | copy-start | bytes 786436
Sparse Core Ops, SparseCore 0:
  10.7 79.5 all-gather.4
  98.2 80.8 reduce-scatter.2
  201.6 73.8 all-gather.2
  283.4 107.7 reduce-scatter.4
where the time goes:
time: 400 us
  waiting for transfers between devices  224 us (56%)
  blocking collectives  57.5 us (14%)
  local copies, waits for them, and re-layouts  49.8 us (12%)
  matrix products  38.7 us (10%)
  between operations  14.1 us (4%)
  other arithmetic  8.78 us (2%)
  starting transfers between devices  6.92 us (2%)
    all_gather x1, waiting for transfers between devices, shards(): weights = lax.all_gather(out_weight, 'row', axis=0, tiled=True)  82.3 us
    all_gather x1, waiting for transfers between devices, shards(): panel = lax.all_gather(gated, 'col', axis=1, tiled=True)  73.7 us
    psum x1, blocking collectives, shards(): lax.psum(local_taps, 'row') * (1.0 / math.sqrt(total_tokens * group))  57.5 us
    reduce_scatter x1, waiting for transfers between devices, shards(): lax.psum_scatter(partial_value.astype(jnp.bfloat16), 'col', scatter_dimen...  44.5 us
    reduce_scatter x1, waiting for transfers between devices, shards(): lax.psum_scatter(lax.dot_general(panel, out_grad, (((0,), (0,)), ((), ())...  20.6 us
    another operation x4, local copies, waits for them, and re-layouts, toeplitz(): tiled = jnp.tile(template, (1, span))  19.6 us
    unnamed x27, local copies, waits for them, and re-layouts  12 us
    dot_general x2, matrix products, convolve(): jnp.einsum('gts,bsgc->btgc', matrix, split, precision=lax.Precision.HIGHEST)  11.9 us
  transfers between devices with their start and end apart: 7, of which 5 were waited for; matrix products, arithmetic and copies ran while one was open for 15% of the time, Pallas kernels for 0%

commit v1 on v0

--- a/solution.py
+++ b/solution.py
@@ -3,6 +3,11 @@
 import jax.numpy as jnp
 from jax import lax
 from jax.sharding import PartitionSpec as P
+from jax.lax import all_gather
+
+
+def keep_up_the_turns(piece_in, ax_name="row"):
+    return jnp.sum(all_gather(piece_in, axis_name=ax_name), 0)
 
 
 def from_behind(shard, axis, by):
@@ -88,7 +93,7 @@
     )
     skewed = flat.reshape(groups, span, 2 * span + 1)[:, :, 1 : span + 1]
     local_taps = jnp.sum(skewed, axis=1)[:, ::-1]
-    filter_grad = lax.psum(local_taps, "row") * (1.0 / math.sqrt(total_tokens * group))
+    filter_grad = keep_up_the_turns(local_taps) * (1.0 / math.sqrt(total_tokens * group))
     weight_sum = lax.psum_scatter(
         lax.dot_general(
             panel, out_grad, (((0,), (0,)), ((), ())), preferred_element_type=f32

time: 400 us -> 400 us (level)
  blocking collectives: 57.5 us -> 22.3 us
  waiting for transfers between devices: 224 us -> 258 us
    psum x1 -> x0, blocking collectives: 57.5 us -> none  [shards(): lax.psum(local_taps, 'row') * (1.0 / math.sqrt(total_tokens * group))]
    reduce_scatter x1, waiting for transfers between devices: 20.6 us -> 55.2 us  [shards(): lax.psum_scatter(lax.dot_general(panel, out_grad, (((0,), (0,)), ((), ())...]
    all_gather x0 -> x1, blocking collectives: none -> 22.3 us  [keep_up_the_turns(): return jnp.sum(all_gather(piece_in, axis_name=ax_name), 0)]
where the time goes in v1:
time: 400 us; the launch traced here: 399 us
  waiting for transfers between devices  258 us (64%)
  local copies, waits for them, and re-layouts  49.8 us (12%)
  matrix products  38.7 us (10%)
  blocking collectives  22.3 us (6%)
  between operations  14.1 us (4%)
  other arithmetic  8.8 us (2%)
  starting transfers between devices  6.92 us (2%)
    all_gather x1, waiting for transfers between devices, shards(): weights = lax.all_gather(out_weight, 'row', axis=0, tiled=True)  82.3 us
    all_gather x1, waiting for transfers between devices, shards(): panel = lax.all_gather(gated, 'col', axis=1, tiled=True)  73.7 us
    reduce_scatter x1, waiting for transfers between devices, shards(): lax.psum_scatter(lax.dot_general(panel, out_grad, (((0,), (0,)), ((), ())...  55.2 us
    reduce_scatter x1, waiting for transfers between devices, shards(): lax.psum_scatter(partial_value.astype(jnp.bfloat16), 'col', scatter_dimen...  44.5 us
    all_gather x1, blocking collectives, keep_up_the_turns(): return jnp.sum(all_gather(piece_in, axis_name=ax_name), 0)  22.3 us
    another operation x4, local copies, waits for them, and re-layouts, toeplitz(): tiled = jnp.tile(template, (1, span))  19.6 us
    unnamed x27, local copies, waits for them, and re-layouts  12 us
    dot_general x2, matrix products, convolve(): jnp.einsum('gts,bsgc->btgc', matrix, split, precision=lax.Precision.HIGHEST)  11.9 us
  transfers between devices with their start and end apart: 7, of which 5 were waited for; matrix products, arithmetic and copies ran while one was open for 15% of the time, Pallas kernels for 0%

profile of v1, /device:TPU:2, one launch (start us, length us, event | category | flops | bytes accessed | tf_op | source)
XLA Modules:
  0.0 399.1 jit_solution(13915365461820113868)
XLA Ops:
  7.2 0.7 all-gather.6.cloned.1.call-update
  8.0 82.3 %all-gather.6.cloned.1.call-done = bf16[8192,512]{1,0:T(8,128)(2,1)} async-done(((bf16[512,512]{1,0:T(8,128)(2,1)}), bf16[8192,512]{1,0:T(8,128)(2,1)}) %all-gather.6.cloned.1.call-update) | async-done | bytes 8388624 | tf_op jit(solution)/shard_map/all_gather | solution.py:68
  90.2 7.8 %convolution_convert_fusion.1 = bf16[256,8192]{1,0:T(8,128)(2,1)} fusion(bf16[256,512]{1,0:T(8,128)(2,1)S(1)} %copy-done, bf16[8192,512]{1,0:T(8,128)(2,1)} %all-gather.6.cloned.1.call-done), kind=kOutput, calls=%fused_computation.1 | convolution fusion | flops 2149580800 | bytes 12845056 | tf_op jit(solution)/shard_map/dot_general | solution.py:70
  98.1 0.9 copy-done.6
  99.2 2.1 collective-permute-start
  101.3 0.1 copy.33
  101.5 2.3 collective-permute-start.1
  103.9 3.1 tile.20
  107.0 6.7 %tile.21 = f32[32,32896]{1,0:T(8,128)} reshape(f32[32,128,257]{2,1,0:T(8,128)} %tile.20) | data formatting | bytes 8421376 | tf_op jit(solution)/shard_map/tile | solution.py:32
  113.7 2.2 slice-done
  115.9 3.3 copy.54
  119.4 3.1 tile.8
  122.5 6.7 %tile.9 = f32[32,32896]{1,0:T(8,128)} reshape(f32[32,128,257]{2,1,0:T(8,128)} %tile.8) | data formatting | bytes 8421376 | tf_op jit(solution)/shard_map/tile | solution.py:32
  129.2 2.2 slice-done.1
  131.4 3.2 copy.52
  134.6 44.5 %reduce-scatter.3.cloned.1.call-done = bf16[256,512]{1,0:T(8,128)(2,1)} async-done(((bf16[256,8192]{1,0:T(8,128)(2,1)}), bf16[256,512]{1,0:T(8,128)(2,1)}) %reduce-scatter.3.cloned.1.call-update) | async-done | bytes 262160 | tf_op jit(solution)/shard_map/reduce_scatter | solution.py:74
  179.1 1.0 convert_multiply_fusion
  180.2 0.7 slice.42
  180.8 2.1 collective-permute-start.2
  183.0 0.2 copy.41
  183.2 0.3 concatenate.37
  183.5 2.0 collective-permute-done.2
  185.6 0.2 copy.42
  185.8 0.3 concatenate.39
  186.2 5.9 %fusion.7 = f32[2,128,32,16]{1,3,0,2:T(8,128)S(1)} fusion(f32[32,128,256,1]{2,1,0,3:T(8,128)} %bitcast.61, f32[2,128,32,16]{1,3,0,2:T(8,128)S(1)} %copy.44, f32[2,128,32,16]{1,3,0,2:T(8,128)S(1)} %copy.43), kind=kOutput, calls=%fused_computation.8 | convolution fusion | flops 402915328 | bytes 5767168 | tf_op jit(solution)/shard_map/gts,bsgc->btgc/dot_general | solution.py:47
  192.1 0.3 copy.45
  192.4 0.9 fusion.14
  193.3 0.3 concatenate.34
  193.6 0.3 concatenate.33
  194.0 5.9 %fusion.4 = f32[2,128,32,16]{1,3,0,2:T(8,128)S(1)} fusion(f32[2,256,32,16]{1,3,0,2:T(8,128)S(1)} %copy_dynamic-update-slice_fusion, f32[32,128,256,1]{2,1,0,3:T(8,128)} %bitcast.60), kind=kOutput, calls=%fused_computation.7 | convolution fusion | flops 402653184 | bytes 5767168 | tf_op jit(solution)/shard_map/gts,bsgc->btgc/dot_general | solution.py:47
  200.0 0.3 copy.38
  200.3 0.2 copy.39
  200.5 0.9 fusion.16
  201.4 0.3 reduce-scatter.5.cloned.1.call-start
  201.7 73.7 %all-gather.4.cloned.1.call-done = bf16[256,8192]{1,0:T(8,128)(2,1)} async-done(((bf16[256,512]{1,0:T(8,128)(2,1)}), bf16[256,8192]{1,0:T(8,128)(2,1)}) %all-gather.4.cloned.1.call-update) | async-done | bytes 4194320 | tf_op jit(solution)/shard_map/all_gather | solution.py:67
  275.4 7.8 %convolution_convert_fusion = bf16[8192,512]{1,0:T(8,128)(2,1)} fusion(bf16[256,8192]{1,0:T(8,128)(2,1)} %all-gather.4.cloned.1.call-done, bf16[256,512]{1,0:T(8,128)(2,1)S(1)} %copy-done), kind=kOutput, calls=%fused_computation | convolution fusion | flops 2151677952 | bytes 12845056 | tf_op jit(solution)/shard_map/dot_general | solution.py:98
  283.2 3.5 fusion.18
  286.7 2.4 copy.56
  289.2 2.3 concatenate.42
  291.5 8.2 %reshape.61 = f32[32,128,257]{2,1,0:T(8,128)} reshape(f32[32,32896]{1,0:T(8,128)} %concatenate.42) | data formatting | bytes 8421376 | tf_op jit(solution)/shard_map/reshape | solution.py:94
  299.7 3.2 slice_reduce_fusion
  303.0 22.3 %all-gather = f32[512,128]{1,0:T(8,128)S(1)} all-gather(f32[32,128]{1,0:T(8,128)S(1)} %rev.7), channel_id=2, replica_groups=mesh['row'=16,'col'=16] {'row'}, dimensions={0}, use_global_device_ids=true | all-gather | bytes 278528 | tf_op jit(solution)/shard_map/all_gather | solution.py:10
  325.4 0.8 copy.47
  326.2 0.8 copy.48
  327.1 0.6 broadcast_multiply_fusion
  327.7 7.8 %convolution_convert_fusion.2 = bf16[256,512]{1,0:T(8,128)(2,1)} fusion(bf16[256,8192]{1,0:T(8,128)(2,1)} %all-gather.4.cloned.1.call-done, bf16[8192,512]{1,0:T(8,128)(2,1)} %all-gather.6.cloned.1.call-done), kind=kOutput, calls=%fused_computation.9 | convolution fusion | flops 2147614720 | bytes 12845056 | tf_op jit(solution)/shard_map/dot_general | solution.py:69
  335.5 55.2 %reduce-scatter.5.cloned.1.call-done = bf16[512,512]{1,0:T(8,128)(2,1)} async-done(((bf16[8192,512]{1,0:T(8,128)(2,1)}), bf16[512,512]{1,0:T(8,128)(2,1)}) %reduce-scatter.5.cloned.1.call-update) | async-done | bytes 524304 | tf_op jit(solution)/shard_map/reduce_scatter | solution.py:97
  390.7 1.9 multiply_convert_fusion
  (47 shorter events, 1.1 us)
Async XLA Ops:
  7.2 83.1 %copy-start = (bf16[256,512]{1,0:T(8,128)(2,1)S(1)}, bf16[256,512]{1,0:T(8,128)(2,1)}, u32[]{:S(2)}) copy-start(bf16[256,512]{1,0:T(8,128)(2,1)} %param.11) | copy-start | bytes 786436
  7.2 83.1 %all-gather.6.cloned.1.call-start = ((), (), s32[]{:S(2)}) async-start(), calls=%async_computation.3 | async-start | bytes 8912896 | tf_op jit(solution)/shard_map/all_gather | solution.py:68
  7.9 171.2 %reduce-scatter.3.cloned.1.call-start = ((), (), s32[]{:S(2)}) async-start(), calls=%async_computation.4 | async-start | bytes 4456448 | tf_op jit(solution)/shard_map/reduce_scatter | solution.py:74
  98.0 0.9 copy-start.6
  98.1 3.2 copy-start.7
  98.1 5.7 %copy-start.8 = (f32[32,128]{1,0:T(8,128)S(1)}, f32[32,128]{1,0:T(8,128)}, u32[]{:S(2)}) copy-start(f32[32,128]{1,0:T(8,128)} %param.9) | copy-start | bytes 49156
  98.1 177.3 %all-gather.4.cloned.1.call-start = ((), (), s32[]{:S(2)}) async-start(), calls=%async_computation.2 | async-start | bytes 4456448 | tf_op jit(solution)/shard_map/all_gather | solution.py:67
  99.2 83.8 %collective-permute-start = (bf16[128,512]{0,1:T(8,128)(2,1)S(1)}, bf16[128,512]{0,1:T(8,128)(2,1)S(1)}, u32[]{:S(2)}, u32[]{:S(2)}) collective-permute-start(bf16[128,512]{0,1:T(8,128)(2,1)S(1)} %slice.34), channel_id=1, source_target_pairs={{0,16},{16,32},{32,48},{48,64},{64,80},{80,96},{96,112},{112,128},... | collective-permute-start | bytes 393224 | tf_op jit(solution)/shard_map/ppermute | solution.py:16
  101.5 81.5 %collective-permute-start.1 = (bf16[128,512]{0,1:T(8,128)(2,1)S(1)}, bf16[128,512]{0,1:T(8,128)(2,1)S(1)}, u32[]{:S(2)}, u32[]{:S(2)}) collective-permute-start(bf16[128,512]{0,1:T(8,128)(2,1)S(1)} %slice.35), channel_id=1, source_target_pairs={{0,16},{16,32},{32,48},{48,64},{64,80},{80,96},{96,112},{112,128},... | collective-permute-start | bytes 393224 | tf_op jit(solution)/shard_map/ppermute | solution.py:16
  113.7 2.2 slice-start
  129.2 2.2 slice-start.1
  131.4 47.7 %copy-start.2 = (bf16[256,512]{1,0:T(8,128)(2,1)S(1)}, bf16[256,512]{1,0:T(8,128)(2,1)}, u32[]{:S(2)}) copy-start(bf16[256,512]{1,0:T(8,128)(2,1)} %param.6) | copy-start | bytes 786436
  180.8 4.7 %collective-permute-start.2 = (bf16[128,512]{1,0:T(8,128)(2,1)}, bf16[128,512]{1,0:T(8,128)(2,1)S(1)}, u32[]{:S(2)}, u32[]{:S(2)}) collective-permute-start(bf16[128,512]{1,0:T(8,128)(2,1)} %slice.42), channel_id=1, source_target_pairs={{16,0},{32,16},{48,32},{64,48},{80,64},{96,80},{112,96},{128,112},... | collective-permute-start | bytes 393224 | tf_op jit(solution)/shard_map/ppermute | solution.py:16
  194.0 6.5 %copy-start.3 = (bf16[256,512]{1,0:T(8,128)(2,1)S(1)}, bf16[256,512]{1,0:T(8,128)(2,1)}, u32[]{:S(2)}) copy-start(bf16[256,512]{1,0:T(8,128)(2,1)} %reduce-scatter.3.cloned.1.call-done) | copy-start | bytes 786436
  201.4 189.2 %reduce-scatter.5.cloned.1.call-start = ((), (), s32[]{:S(2)}) async-start(), calls=%async_computation.5 | async-start | bytes 8912896 | tf_op jit(solution)/shard_map/reduce_scatter | solution.py:97
  291.5 33.9 %copy-start.5 = (bf16[256,512]{0,1:T(8,128)(2,1)S(1)}, bf16[256,512]{0,1:T(8,128)(2,1)}, u32[]{:S(2)}) copy-start(bf16[256,512]{0,1:T(8,128)(2,1)} %get-tuple-element.19) | copy-start | bytes 786436
  291.5 34.7 %copy-start.4 = (bf16[256,512]{0,1:T(8,128)(2,1)S(1)}, bf16[256,512]{0,1:T(8,128)(2,1)}, u32[]{:S(2)}) copy-start(bf16[256,512]{0,1:T(8,128)(2,1)} %get-tuple-element.18) | copy-start | bytes 786436
  327.7 64.9 %copy-start.1 = (bf16[256,512]{1,0:T(8,128)(2,1)S(1)}, bf16[256,512]{1,0:T(8,128)(2,1)}, u32[]{:S(2)}) copy-start(bf16[256,512]{1,0:T(8,128)(2,1)} %param.11) | copy-start | bytes 786436
Sparse Core Ops, SparseCore 0:
  10.7 79.5 all-gather.5
  98.2 80.8 reduce-scatter.2
  201.6 73.8 all-gather.3
  283.4 107.2 reduce-scatter.4
